TPU v7x, 32 devices: a whole 2x2x4 slice. The times are simulated.
32 devices in a mesh: fsdp: 8 (over z, x), rep: 2 (over y), ctx: 2 (over core).
Axes of the slice: x: 2, y: 2, z: 4, core: 2. Of those that a mesh axis runs over, the one named last changes fastest.
Arguments:
- tokens: bfloat16 [16, 2048, 768], P(('fsdp', 'rep'), 'ctx'), may hold values from -10 to 10
- cotangent: bfloat16 [16, 2048, 768], P(('fsdp', 'rep'), 'ctx'), may hold values from -6 to 6
- doc_lengths: int32 [16, 4], P(('fsdp', 'rep')), may hold values from 1 to 1024, 2048 in all within a row
- attn_gain: bfloat16 [768], replicated, may hold values from 0.5 to 1.5
- qkv_weight: bfloat16 [768, 2304], P('fsdp'), may hold values from -1 to 1
- out_weight: bfloat16 [768, 768], P('fsdp'), may hold values from -1.75 to 1.75
- mlp_gain: bfloat16 [768], replicated, may hold values from 0.5 to 1.5
- in_weight: bfloat16 [768, 2304], P('fsdp'), may hold values from -0.21875 to 0.21875
- down_weight: bfloat16 [1152, 768], P('fsdp'), may hold values from -0.1875 to 0.1875
Outputs:
- output: bfloat16 [16, 2048, 768], P(('fsdp', 'rep'), 'ctx')
- input_grad: float32 [16, 2048, 768], P(('fsdp', 'rep'), 'ctx')
- grad_attn_gain: float32 [768], replicated
- grad_qkv: float32 [768, 2304], P('fsdp')
- grad_out: float32 [768, 768], P('fsdp')
- grad_mlp_gain: float32 [768], replicated
- grad_in: float32 [768, 2304], P('fsdp')
- grad_down: float32 [1152, 768], P('fsdp')
Inputs may be any that keep to these rules, and one draw needn't show every extreme that they name: `doc_lengths`: the 4 lengths of a row sum to 2048; in every row the longest is exactly 1024.
All inputs are finite; a program needn't handle non-finite values.
Results may differ from a plain program's by a relative error of at most 0.038.
Values may be sent and summed in bfloat16 or wider, within the bound.
A program may use at most 256 MiB of HBM per device.

v0:
```python
import math

import jax
import jax.numpy as jnp
from jax import lax
from jax.sharding import PartitionSpec as P

D = 768
FF = 1152
HEADS = 12
HD = 64
LEN = 2048


norm_eps = 1e-05
rope_base = 160000.0
masked_score = -1e30


def layer_norm(values):
    center = values - jnp.mean(values, axis=-1, keepdims=True)
    inverse = lax.rsqrt(jnp.mean(center * center, axis=-1, keepdims=True) + norm_eps)
    return (center * inverse, inverse)


def norm_back(grad_normed, normed, inverse):
    mean_grad = jnp.mean(grad_normed, axis=-1, keepdims=True)
    mean_cross = jnp.mean(grad_normed * normed, axis=-1, keepdims=True)
    return (grad_normed - mean_grad - normed * mean_cross) * inverse


def gelu_pair(values):
    cumulative = 0.5 * (1.0 + lax.erf(values * 0.7071067811865476))
    density = jnp.exp(-0.5 * values * values) * 0.3989422804014327
    return (values * cumulative, cumulative + values * density)


def doc_tables(lengths, positions):
    doc_ends = jnp.cumsum(lengths)
    before = (doc_ends[None, :] <= positions[:, None]).astype(jnp.int32)
    segment = jnp.sum(before, axis=1)
    begins = jnp.sum(before * lengths[None, :], axis=1)
    return (segment, positions - begins)


def rope_tables(offsets, head_size):
    half_size = head_size // 2
    frequency = rope_base ** (-(jnp.arange(half_size, dtype=jnp.float32) * (2.0 / head_size)))
    angles = offsets.astype(jnp.float32)[..., None] * frequency
    return (jnp.cos(angles), jnp.sin(angles))


def rotate(values, cosine, sine_part):
    half_size = values.shape[-1] // 2
    leading, trailing = (values[..., :half_size], values[..., half_size:])
    cos_head, sin_head = (cosine[..., None, :], sine_part[..., None, :])
    return jnp.concatenate(
        [leading * cos_head - trailing * sin_head, trailing * cos_head + leading * sin_head],
        axis=-1,
    )


def unrotate(gradient, cosine, sine_part):
    half_size = gradient.shape[-1] // 2
    leading, trailing = (gradient[..., :half_size], gradient[..., half_size:])
    cos_head, sin_head = (cosine[..., None, :], sine_part[..., None, :])
    return jnp.concatenate(
        [leading * cos_head + trailing * sin_head, trailing * cos_head - leading * sin_head],
        axis=-1,
    )


def project(activations, weight):
    return jnp.dot(
        activations,
        lax.all_gather(weight, "fsdp", axis=0, tiled=True),
        preferred_element_type=jnp.float32,
    )


def project_back(gradient, weight):
    return lax.dot_general(
        gradient,
        lax.all_gather(weight, "fsdp", axis=0, tiled=True),
        (((1,), (1,)), ((), ())),
        preferred_element_type=jnp.float32,
    )


def weight_grad(activations, gradient):
    shard_sum = lax.psum_scatter(
        lax.dot_general(
            activations, gradient, (((0,), (0,)), ((), ())), preferred_element_type=jnp.float32
        ).astype(jnp.bfloat16),
        "fsdp",
        scatter_dimension=0,
        tiled=True,
    ).astype(jnp.float32)
    shard_sum = lax.psum(shard_sum.astype(jnp.bfloat16), ("rep", "ctx")).astype(jnp.float32)
    return shard_sum


def score_block(query_rows, key_rows, seg_rows, seg_keys, score_scale):
    scores = (
        jnp.einsum("rqhd,rkhd->rhqk", query_rows, key_rows, preferred_element_type=jnp.float32)
        * score_scale
    )
    allowed = (seg_rows[:, :, None] == seg_keys[:, None, :])[:, None]
    return (jnp.where(allowed, scores, masked_score), allowed)


def split_pair(kv_block, rows_here):
    key_block = kv_block[..., :D].reshape(rows_here, kv_block.shape[1], HEADS, HD)
    value_block = kv_block[..., D:].reshape(rows_here, kv_block.shape[1], HEADS, HD)
    return (key_block, value_block)


def per_device(
    tokens,
    cotangent,
    doc_lengths,
    attn_gain,
    qkv_weight,
    out_weight,
    mlp_gain,
    in_weight,
    down_weight,
):
    rows_here = tokens.shape[0]
    block_len = tokens.shape[1]
    flat_count = rows_here * block_len
    score_scale = HD ** (-0.5)
    first_pos = lax.axis_index("ctx") * block_len
    local_pos = first_pos + jnp.arange(block_len, dtype=jnp.int32)
    all_pos = jnp.arange(LEN, dtype=jnp.int32)
    seg_all, unused_offsets = jax.vmap(doc_tables, in_axes=(0, None))(doc_lengths, all_pos)
    seg_query, offsets = jax.vmap(doc_tables, in_axes=(0, None))(doc_lengths, local_pos)
    cosine, sine_part = rope_tables(offsets, HD)
    inputs = tokens.reshape(flat_count, D).astype(jnp.float32)
    normed_attn, inverse_attn = layer_norm(inputs)
    act_attn = (normed_attn * attn_gain.astype(jnp.float32)).astype(jnp.bfloat16)
    qkv_all = project(act_attn, qkv_weight)
    shaped = (rows_here, block_len, HEADS, HD)
    query = rotate(qkv_all[:, :D].reshape(shaped), cosine, sine_part).astype(jnp.bfloat16)
    key_local = rotate(qkv_all[:, D : 2 * D].reshape(shaped), cosine, sine_part).astype(
        jnp.bfloat16
    )
    value_local = qkv_all[:, 2 * D :].astype(jnp.bfloat16)
    kv_local = jnp.concatenate(
        [key_local.reshape(rows_here, block_len, D), value_local.reshape(rows_here, block_len, D)],
        axis=-1,
    )

    def step_block(state, kv_block, seg_key):
        run_max, run_sum, accum = state
        key_block, value_block = split_pair(kv_block, rows_here)
        scores, allowed = score_block(query, key_block, seg_query, seg_key, score_scale)
        new_max = jnp.maximum(run_max, jnp.max(scores, axis=-1))
        weights = jnp.where(allowed, jnp.exp(scores - new_max[..., None]), 0.0)
        factor = jnp.exp(run_max - new_max)
        new_sum = run_sum * factor + jnp.sum(weights, axis=-1)
        new_acc = accum * factor[..., None] + jnp.einsum(
            "rhqk,rkhd->rhqd",
            weights.astype(jnp.bfloat16),
            value_block,
            preferred_element_type=jnp.float32,
        )
        return (new_max, new_sum, new_acc)

    initial = (
        jnp.full((rows_here, HEADS, block_len), masked_score, jnp.float32),
        jnp.zeros((rows_here, HEADS, block_len), jnp.float32),
        jnp.zeros((rows_here, HEADS, block_len, HD), jnp.float32),
    )
    kv_piece = lax.all_gather(kv_local, "ctx", axis=1, tiled=True)
    sub_len = math.gcd(kv_piece.shape[1], 512)

    def inner_step(carry, index):
        kv_block = lax.dynamic_slice_in_dim(kv_piece, index * sub_len, sub_len, 1)
        seg_key = lax.dynamic_slice_in_dim(seg_all, index * sub_len, sub_len, 1)
        return (step_block(carry, kv_block, seg_key), None)

    state = lax.scan(
        inner_step, initial, jnp.arange(kv_piece.shape[1] // sub_len, dtype=jnp.int32)
    )[0]
    run_max, run_sum, accum = state
    log_total = run_max + jnp.log(run_sum)
    attended = jnp.transpose(accum / run_sum[..., None], (0, 2, 1, 3)).astype(jnp.bfloat16)
    att_flat = attended.reshape(flat_count, D)
    residual = inputs + project(att_flat, out_weight)
    normed_mlp, inverse_mlp = layer_norm(residual)
    act_mlp = (normed_mlp * mlp_gain.astype(jnp.float32)).astype(jnp.bfloat16)
    up_all = project(act_mlp, in_weight)
    inner, gate = (up_all[:, :FF], up_all[:, FF:])
    gelu_value, gelu_slope = gelu_pair(inner)
    mixed = (gelu_value * gate).astype(jnp.bfloat16)
    output = (residual + project(mixed, down_weight)).astype(jnp.bfloat16)
    cot_flat = cotangent.reshape(flat_count, D)
    grad_down = weight_grad(mixed, cot_flat)
    d_mixed = project_back(cot_flat, down_weight)
    d_up = jnp.concatenate([d_mixed * gate * gelu_slope, d_mixed * gelu_value], axis=-1).astype(
        jnp.bfloat16
    )
    grad_in = weight_grad(act_mlp, d_up)
    d_act_mlp = project_back(d_up, in_weight)
    local_mlp_gain = jnp.sum(d_act_mlp * normed_mlp, axis=0)
    d_residual = cot_flat.astype(jnp.float32) + norm_back(
        d_act_mlp * mlp_gain.astype(jnp.float32), normed_mlp, inverse_mlp
    )
    d_res_half = d_residual.astype(jnp.bfloat16)
    grad_out = weight_grad(att_flat, d_res_half)
    d_att = project_back(d_res_half, out_weight).astype(jnp.bfloat16).reshape(shaped)
    kv_all = lax.all_gather(kv_local, "ctx", axis=1, tiled=True)
    delta = jnp.transpose(
        jnp.sum(d_att.astype(jnp.float32) * attended.astype(jnp.float32), axis=-1), (0, 2, 1)
    )
    key_len = math.gcd(LEN, 512)
    key_count = LEN // key_len

    def block_parts(index):
        kv_block = lax.dynamic_slice_in_dim(kv_all, index * key_len, key_len, 1)
        seg_key = lax.dynamic_slice_in_dim(seg_all, index * key_len, key_len, 1)
        key_block, value_block = split_pair(kv_block, rows_here)
        scores, allowed = score_block(query, key_block, seg_query, seg_key, score_scale)
        probs = jnp.where(allowed, jnp.exp(scores - log_total[..., None]), 0.0)
        d_probs = jnp.einsum(
            "rqhd,rkhd->rhqk", d_att, value_block, preferred_element_type=jnp.float32
        )
        d_scores = (probs * (d_probs - delta[..., None])).astype(jnp.bfloat16)
        return (probs.astype(jnp.bfloat16), d_scores, key_block)

    zero_query = jnp.zeros(shaped, jnp.float32)

    def both_step(running, index):
        probs_half, d_scores, key_block = block_parts(index)
        added = (
            jnp.einsum("rhqk,rkhd->rqhd", d_scores, key_block, preferred_element_type=jnp.float32)
            * score_scale
        )
        key_part = (
            jnp.einsum("rhqk,rqhd->krhd", d_scores, query, preferred_element_type=jnp.float32)
            * score_scale
        )
        value_part = jnp.einsum(
            "rhqk,rqhd->krhd", probs_half, d_att, preferred_element_type=jnp.float32
        )
        pair_part = jnp.concatenate(
            [key_part.reshape(key_len, rows_here, D), value_part.reshape(key_len, rows_here, D)],
            axis=-1,
        )
        return (running + added, pair_part)

    query_grad, pair_blocks = lax.scan(
        both_step, zero_query, jnp.arange(key_count, dtype=jnp.int32)
    )
    pair_terms = pair_blocks.reshape(LEN, rows_here, 2 * D)
    pair_grad = jnp.transpose(
        lax.psum_scatter(
            pair_terms.astype(jnp.bfloat16), "ctx", scatter_dimension=0, tiled=True
        ).astype(jnp.float32),
        (1, 0, 2),
    )
    key_grad_here = pair_grad[..., :D].reshape(shaped)
    value_grad_here = pair_grad[..., D:].reshape(flat_count, D)
    key_grad = unrotate(key_grad_here, cosine, sine_part).reshape(flat_count, D)
    query_flat = unrotate(query_grad, cosine, sine_part).reshape(flat_count, D)
    d_qkv = jnp.concatenate([query_flat, key_grad, value_grad_here], axis=-1).astype(jnp.bfloat16)
    grad_qkv = weight_grad(act_attn, d_qkv)
    d_act_attn = project_back(d_qkv, qkv_weight)
    local_attn_gain = jnp.sum(d_act_attn * normed_attn, axis=0)
    input_grad = d_residual + norm_back(
        d_act_attn * attn_gain.astype(jnp.float32), normed_attn, inverse_attn
    )
    grad_attn_gain, grad_mlp_gain = lax.psum(
        (local_attn_gain, local_mlp_gain), ("fsdp", "rep", "ctx")
    )
    return (
        output.reshape(rows_here, block_len, D),
        input_grad.reshape(rows_here, block_len, D),
        grad_attn_gain,
        grad_qkv,
        grad_out,
        grad_mlp_gain,
        grad_in,
        grad_down,
    )


def solution(mesh):
    return jax.shard_map(
        per_device,
        mesh=mesh,
        in_specs=(
            P(("fsdp", "rep"), "ctx", None),
            P(("fsdp", "rep"), "ctx", None),
            P(("fsdp", "rep"), None),
            P(),
            P("fsdp", None),
            P("fsdp", None),
            P(),
            P("fsdp", None),
            P("fsdp", None),
        ),
        out_specs=(
            P(("fsdp", "rep"), "ctx", None),
            P(("fsdp", "rep"), "ctx", None),
            P(),
            P("fsdp", None),
            P("fsdp", None),
            P(),
            P("fsdp", None),
            P("fsdp", None),
        ),
        check_vma=False,
    )
```

profile of v0, /device:TPU:0, one launch (start us, length us, event | category | flops | bytes accessed | tf_op | source)
XLA Modules:
  0.0 971.2 jit_solution(4961686260526248050)
XLA Ops:
  12.0 65.5 %all-gather.6.cloned.1.call-done = bf16[768,2304]{1,0:T(8,128)(2,1)} async-done(((bf16[96,2304]{1,0:T(8,128)(2,1)}), bf16[768,2304]{1,0:T(8,128)(2,1)}) %all-gather.6.cloned.1.call-update) | async-done | bytes 3538960 | tf_op jit(solution)/shard_map/all_gather | solution.py:76
  107.8 10.9 %all-gather.8.cloned.1.call-done = bf16[1,2048,1536]{2,1,0:T(8,128)(2,1)} async-done(((bf16[1,1024,1536]{2,1,0:T(8,128)(2,1)}), bf16[1,2048,1536]{2,1,0:T(8,128)(2,1)}) %all-gather.8.cloned.1.call-update) | async-done | bytes 6291472 | tf_op jit(solution)/shard_map/all_gather | solution.py:175
  118.7 8.8 copy.59
  127.5 156.9 %while.28 = (s32[]{:T(128)}, f32[1,12,1024]{2,1,0:T(8,128)S(1)}, f32[1,12,1024]{2,1,0:T(8,128)S(1)}, f32[1,12,1024,64]{2,3,1,0:T(8,128)}, s32[1,1024]{1,0:T(1,12...) while((s32[]{:T(128)}, f32[1,12,1024]{2,1,0:T(8,128)S(1)}, ...), condition=%wide.region_9.10_spmd.clone, body=%wide.region_6.9_spmd.clone.sunk | while | flops 1695358976 | bytes 116140320 | solution.py:183
  130.6 10.6 %fusion.119 = (f32[12,1024]{1,0:T(8,128)S(1)}, f32[12,512,1024]{2,1,0:T(8,128)}) fusion(pred[1024,512]{0,1:T(8,128)(4,1)S(1)} %broadcast_compare_fusion.4, bf16[512,12,64]{0,2,1:T(8,128)(2,1)S(1)} %bitcast.262, bf16[1,1024,12,64]{1,3,2,0:T(8,128)(2,1)S(1)} %get-tuple-element.533), kind=kOutput, calls=%fused_computation.2.clone.1 | convolution fusion | flops 824168448 | bytes 28098560 | tf_op jit(solution)/shard_map/while/body/eval_jaxpr/rqhd,rkhd->rhqk/dot_general | solution.py:105
  141.2 11.7 %fusion.121 = f32[12,1024]{1,0:T(8,128)S(1)} fusion(f32[12,512,1024]{2,1,0:T(8,128)} %get-tuple-element.481, f32[12,1024]{1,0:T(8,128)S(1)} %bitcast.263, pred[1024,512]{0,1:T(8,128)(4,1)S(1)} %broadcast_compare_fusion.4), kind=kLoop, calls=%fused_computation.4.clone.1 | loop fusion | flops 31444992 | bytes 25788416 | tf_op jit(solution)/shard_map/while/body/eval_jaxpr/reduce_sum | solution.py:161
  153.0 11.8 %bitcast_add_fusion.7 = f32[1,12,1024,64]{2,3,1,0:T(8,128)S(1)} fusion(f32[1,12,1024,64]{2,3,1,0:T(8,128)S(1)} %copy-done.7, bf16[512,12,64]{0,2,1:T(8,128)(2,1)S(1)} %bitcast.265, f32[12,512,1024]{2,1,0:T(8,128)} %get-tuple-element.481, f32[12,1024]{1,0:T(8,128)S(1)} %bitcast.264, pred[1024,512]{0,1:T(8,128)(4,1)S(1)} %broadcast_compare_fusion.4, ...), kind=kOutput, calls=%fused_computation.7.clone.1 | convolution fusion | flops 839122944 | bytes 32866304 | tf_op jit(solution)/shard_map/while/body/eval_jaxpr/rhqk,rkhd->rhqd/dot_general | solution.py:162
  169.6 10.6 %fusion.119 = (f32[12,1024]{1,0:T(8,128)S(1)}, f32[12,512,1024]{2,1,0:T(8,128)}) fusion(pred[1024,512]{0,1:T(8,128)(4,1)S(1)} %broadcast_compare_fusion.4, bf16[512,12,64]{0,2,1:T(8,128)(2,1)S(1)} %bitcast.262, bf16[1,1024,12,64]{1,3,2,0:T(8,128)(2,1)S(1)} %get-tuple-element.533), kind=kOutput, calls=%fused_computation.2.clone.1 | convolution fusion | flops 824168448 | bytes 28098560 | tf_op jit(solution)/shard_map/while/body/eval_jaxpr/rqhd,rkhd->rhqk/dot_general | solution.py:105
  180.2 11.6 %fusion.121 = f32[12,1024]{1,0:T(8,128)S(1)} fusion(f32[12,512,1024]{2,1,0:T(8,128)} %get-tuple-element.481, f32[12,1024]{1,0:T(8,128)S(1)} %bitcast.263, pred[1024,512]{0,1:T(8,128)(4,1)S(1)} %broadcast_compare_fusion.4), kind=kLoop, calls=%fused_computation.4.clone.1 | loop fusion | flops 31444992 | bytes 25788416 | tf_op jit(solution)/shard_map/while/body/eval_jaxpr/reduce_sum | solution.py:161
  191.9 12.2 %bitcast_add_fusion.7 = f32[1,12,1024,64]{2,3,1,0:T(8,128)S(1)} fusion(f32[1,12,1024,64]{2,3,1,0:T(8,128)S(1)} %copy-done.7, bf16[512,12,64]{0,2,1:T(8,128)(2,1)S(1)} %bitcast.265, f32[12,512,1024]{2,1,0:T(8,128)} %get-tuple-element.481, f32[12,1024]{1,0:T(8,128)S(1)} %bitcast.264, pred[1024,512]{0,1:T(8,128)(4,1)S(1)} %broadcast_compare_fusion.4, ...), kind=kOutput, calls=%fused_computation.7.clone.1 | convolution fusion | flops 839122944 | bytes 32866304 | tf_op jit(solution)/shard_map/while/body/eval_jaxpr/rhqk,rkhd->rhqd/dot_general | solution.py:162
  208.9 10.7 %fusion.119 = (f32[12,1024]{1,0:T(8,128)S(1)}, f32[12,512,1024]{2,1,0:T(8,128)}) fusion(pred[1024,512]{0,1:T(8,128)(4,1)S(1)} %broadcast_compare_fusion.4, bf16[512,12,64]{0,2,1:T(8,128)(2,1)S(1)} %bitcast.262, bf16[1,1024,12,64]{1,3,2,0:T(8,128)(2,1)S(1)} %get-tuple-element.533), kind=kOutput, calls=%fused_computation.2.clone.1 | convolution fusion | flops 824168448 | bytes 28098560 | tf_op jit(solution)/shard_map/while/body/eval_jaxpr/rqhd,rkhd->rhqk/dot_general | solution.py:105
  219.7 11.6 %fusion.121 = f32[12,1024]{1,0:T(8,128)S(1)} fusion(f32[12,512,1024]{2,1,0:T(8,128)} %get-tuple-element.481, f32[12,1024]{1,0:T(8,128)S(1)} %bitcast.263, pred[1024,512]{0,1:T(8,128)(4,1)S(1)} %broadcast_compare_fusion.4), kind=kLoop, calls=%fused_computation.4.clone.1 | loop fusion | flops 31444992 | bytes 25788416 | tf_op jit(solution)/shard_map/while/body/eval_jaxpr/reduce_sum | solution.py:161
  231.3 12.0 %bitcast_add_fusion.7 = f32[1,12,1024,64]{2,3,1,0:T(8,128)S(1)} fusion(f32[1,12,1024,64]{2,3,1,0:T(8,128)S(1)} %copy-done.7, bf16[512,12,64]{0,2,1:T(8,128)(2,1)S(1)} %bitcast.265, f32[12,512,1024]{2,1,0:T(8,128)} %get-tuple-element.481, f32[12,1024]{1,0:T(8,128)S(1)} %bitcast.264, pred[1024,512]{0,1:T(8,128)(4,1)S(1)} %broadcast_compare_fusion.4, ...), kind=kOutput, calls=%fused_computation.7.clone.1 | convolution fusion | flops 839122944 | bytes 32866304 | tf_op jit(solution)/shard_map/while/body/eval_jaxpr/rhqk,rkhd->rhqd/dot_general | solution.py:162
  248.1 10.8 %fusion.119 = (f32[12,1024]{1,0:T(8,128)S(1)}, f32[12,512,1024]{2,1,0:T(8,128)}) fusion(pred[1024,512]{0,1:T(8,128)(4,1)S(1)} %broadcast_compare_fusion.4, bf16[512,12,64]{0,2,1:T(8,128)(2,1)S(1)} %bitcast.262, bf16[1,1024,12,64]{1,3,2,0:T(8,128)(2,1)S(1)} %get-tuple-element.533), kind=kOutput, calls=%fused_computation.2.clone.1 | convolution fusion | flops 824168448 | bytes 28098560 | tf_op jit(solution)/shard_map/while/body/eval_jaxpr/rqhd,rkhd->rhqk/dot_general | solution.py:105
  258.9 11.7 %fusion.121 = f32[12,1024]{1,0:T(8,128)S(1)} fusion(f32[12,512,1024]{2,1,0:T(8,128)} %get-tuple-element.481, f32[12,1024]{1,0:T(8,128)S(1)} %bitcast.263, pred[1024,512]{0,1:T(8,128)(4,1)S(1)} %broadcast_compare_fusion.4), kind=kLoop, calls=%fused_computation.4.clone.1 | loop fusion | flops 31444992 | bytes 25788416 | tf_op jit(solution)/shard_map/while/body/eval_jaxpr/reduce_sum | solution.py:161
  270.6 11.8 %bitcast_add_fusion.7 = f32[1,12,1024,64]{2,3,1,0:T(8,128)S(1)} fusion(f32[1,12,1024,64]{2,3,1,0:T(8,128)S(1)} %copy-done.7, bf16[512,12,64]{0,2,1:T(8,128)(2,1)S(1)} %bitcast.265, f32[12,512,1024]{2,1,0:T(8,128)} %get-tuple-element.481, f32[12,1024]{1,0:T(8,128)S(1)} %bitcast.264, pred[1024,512]{0,1:T(8,128)(4,1)S(1)} %broadcast_compare_fusion.4, ...), kind=kOutput, calls=%fused_computation.7.clone.1 | convolution fusion | flops 839122944 | bytes 32866304 | tf_op jit(solution)/shard_map/while/body/eval_jaxpr/rhqk,rkhd->rhqd/dot_general | solution.py:162
  293.4 10.7 %fusion.74 = f32[1024,2304]{1,0:T(8,128)} fusion(bf16[768,2304]{1,0:T(8,128)(2,1)} %all-gather.12.cloned.1.call-done, f32[1024,768]{0,1:T(8,128)} %copy-done.10, f32[768]{0:T(1024)S(1)} %copy-done.36, f32[1024]{0:T(1024)S(1)} %add_rsqrt_fusion, f32[1024]{0:T(1024)S(1)} %broadcast_multiply_fusion.4), kind=kOutput, calls=%fused_computation.146 | convolution fusion | flops 3627024384 | bytes 16133120 | tf_op jit(solution)/shard_map/dot_general | solution.py:74
  304.2 8.9 fusion.39
  323.0 265.3 %while.29 = (s32[]{:T(128)}, f32[1,1024,12,64]{1,3,2,0:T(8,128)}, bf16[4,512,1,1536]{3,1,0,2:T(8,128)(2,1)}, s32[4]{0:T(128)S(1)}, bf16[1,2048,1536]{1,2,0:T(8,1...) while((s32[]{:T(128)}, f32[1,1024,12,64]{1,3,2,0:T(8,128)}, ...), condition=%wide.region_16.17_spmd.clone, body=%wide.region_15.16_spmd.clone.sunk | while | flops 4108845056 | bytes 165046672 | solution.py:253
  326.6 10.1 %fusion.132 = f32[12,512,1024]{2,1,0:T(8,128)} fusion(bf16[512,12,64]{0,2,1:T(8,128)(2,1)S(1)} %bitcast.260, bf16[1,1024,12,64]{1,3,2,0:T(8,128)(2,1)S(1)} %get-tuple-element.578), kind=kOutput, calls=%fused_computation.38.clone.1 | convolution fusion | flops 805306368 | bytes 27525120 | tf_op jit(solution)/shard_map/while/body/eval_jaxpr/rqhd,rkhd->rhqk/dot_general | solution.py:105
  336.8 12.4 %fusion.134 = bf16[12,512,64]{1,2,0:T(8,128)(2,1)} fusion(f32[12,512,1024]{2,1,0:T(8,128)} %fusion.132, f32[12,1024]{1,0:T(8,128)S(1)} %bitcast.291, pred[1024,512]{0,1:T(8,128)(4,1)S(1)} %broadcast_compare_fusion.5, bf16[1,1024,12,64]{1,3,2,0:T(8,128)(2,1)} %copy-done.22), kind=kOutput, calls=%fused_computation.30.clone.1 | convolution fusion | flops 836763648 | bytes 28098560 | tf_op jit(solution)/shard_map/while/body/eval_jaxpr/rhqk,rqhd->krhd/dot_general | solution.py:244
  349.2 17.0 %fusion.133 = bf16[12,1024,512]{1,2,0:T(8,128)(2,1)} fusion(f32[12,512,1024]{2,1,0:T(8,128)} %fusion.132, f32[12,1024]{1,0:T(8,128)S(1)} %bitcast.290, f32[12,1024]{1,0:T(8,128)S(1)} %bitcast.292, pred[1024,512]{0,1:T(8,128)(4,1)} %copy-done.6, bf16[512,12,64]{0,2,1:T(8,128)(2,1)S(1)} %bitcast.267, bf16[1,1024,12,64]{1,3,2,0:T(8,128)(2,1)} %copy-done.22), kind=kOutput, calls=%fused_computation.24.clone.1 | convolution fusion | flops 849346560 | bytes 40730624 | tf_op jit(solution)/shard_map/while/body/eval_jaxpr/rqhd,rkhd->rhqk/dot_general | solution.py:226
  366.2 9.4 fusion.135
  375.6 8.7 bitcast_add_fusion.8
  392.2 10.1 %fusion.132 = f32[12,512,1024]{2,1,0:T(8,128)} fusion(bf16[512,12,64]{0,2,1:T(8,128)(2,1)S(1)} %bitcast.260, bf16[1,1024,12,64]{1,3,2,0:T(8,128)(2,1)S(1)} %get-tuple-element.578), kind=kOutput, calls=%fused_computation.38.clone.1 | convolution fusion | flops 805306368 | bytes 27525120 | tf_op jit(solution)/shard_map/while/body/eval_jaxpr/rqhd,rkhd->rhqk/dot_general | solution.py:105
  402.3 12.4 %fusion.134 = bf16[12,512,64]{1,2,0:T(8,128)(2,1)} fusion(f32[12,512,1024]{2,1,0:T(8,128)} %fusion.132, f32[12,1024]{1,0:T(8,128)S(1)} %bitcast.291, pred[1024,512]{0,1:T(8,128)(4,1)S(1)} %broadcast_compare_fusion.5, bf16[1,1024,12,64]{1,3,2,0:T(8,128)(2,1)} %copy-done.22), kind=kOutput, calls=%fused_computation.30.clone.1 | convolution fusion | flops 836763648 | bytes 28098560 | tf_op jit(solution)/shard_map/while/body/eval_jaxpr/rhqk,rqhd->krhd/dot_general | solution.py:244
  414.7 17.0 %fusion.133 = bf16[12,1024,512]{1,2,0:T(8,128)(2,1)} fusion(f32[12,512,1024]{2,1,0:T(8,128)} %fusion.132, f32[12,1024]{1,0:T(8,128)S(1)} %bitcast.290, f32[12,1024]{1,0:T(8,128)S(1)} %bitcast.292, pred[1024,512]{0,1:T(8,128)(4,1)} %copy-done.6, bf16[512,12,64]{0,2,1:T(8,128)(2,1)S(1)} %bitcast.267, bf16[1,1024,12,64]{1,3,2,0:T(8,128)(2,1)} %copy-done.22), kind=kOutput, calls=%fused_computation.24.clone.1 | convolution fusion | flops 849346560 | bytes 40730624 | tf_op jit(solution)/shard_map/while/body/eval_jaxpr/rqhd,rkhd->rhqk/dot_general | solution.py:226
  431.7 9.4 fusion.135
  441.1 9.6 bitcast_add_fusion.8
  458.6 10.1 %fusion.132 = f32[12,512,1024]{2,1,0:T(8,128)} fusion(bf16[512,12,64]{0,2,1:T(8,128)(2,1)S(1)} %bitcast.260, bf16[1,1024,12,64]{1,3,2,0:T(8,128)(2,1)S(1)} %get-tuple-element.578), kind=kOutput, calls=%fused_computation.38.clone.1 | convolution fusion | flops 805306368 | bytes 27525120 | tf_op jit(solution)/shard_map/while/body/eval_jaxpr/rqhd,rkhd->rhqk/dot_general | solution.py:105
  468.8 12.4 %fusion.134 = bf16[12,512,64]{1,2,0:T(8,128)(2,1)} fusion(f32[12,512,1024]{2,1,0:T(8,128)} %fusion.132, f32[12,1024]{1,0:T(8,128)S(1)} %bitcast.291, pred[1024,512]{0,1:T(8,128)(4,1)S(1)} %broadcast_compare_fusion.5, bf16[1,1024,12,64]{1,3,2,0:T(8,128)(2,1)} %copy-done.22), kind=kOutput, calls=%fused_computation.30.clone.1 | convolution fusion | flops 836763648 | bytes 28098560 | tf_op jit(solution)/shard_map/while/body/eval_jaxpr/rhqk,rqhd->krhd/dot_general | solution.py:244
  481.2 17.0 %fusion.133 = bf16[12,1024,512]{1,2,0:T(8,128)(2,1)} fusion(f32[12,512,1024]{2,1,0:T(8,128)} %fusion.132, f32[12,1024]{1,0:T(8,128)S(1)} %bitcast.290, f32[12,1024]{1,0:T(8,128)S(1)} %bitcast.292, pred[1024,512]{0,1:T(8,128)(4,1)} %copy-done.6, bf16[512,12,64]{0,2,1:T(8,128)(2,1)S(1)} %bitcast.267, bf16[1,1024,12,64]{1,3,2,0:T(8,128)(2,1)} %copy-done.22), kind=kOutput, calls=%fused_computation.24.clone.1 | convolution fusion | flops 849346560 | bytes 40730624 | tf_op jit(solution)/shard_map/while/body/eval_jaxpr/rqhd,rkhd->rhqk/dot_general | solution.py:226
  498.2 9.4 fusion.135
  507.6 9.6 bitcast_add_fusion.8
  525.1 10.1 %fusion.132 = f32[12,512,1024]{2,1,0:T(8,128)} fusion(bf16[512,12,64]{0,2,1:T(8,128)(2,1)S(1)} %bitcast.260, bf16[1,1024,12,64]{1,3,2,0:T(8,128)(2,1)S(1)} %get-tuple-element.578), kind=kOutput, calls=%fused_computation.38.clone.1 | convolution fusion | flops 805306368 | bytes 27525120 | tf_op jit(solution)/shard_map/while/body/eval_jaxpr/rqhd,rkhd->rhqk/dot_general | solution.py:105
  535.2 12.4 %fusion.134 = bf16[12,512,64]{1,2,0:T(8,128)(2,1)} fusion(f32[12,512,1024]{2,1,0:T(8,128)} %fusion.132, f32[12,1024]{1,0:T(8,128)S(1)} %bitcast.291, pred[1024,512]{0,1:T(8,128)(4,1)S(1)} %broadcast_compare_fusion.5, bf16[1,1024,12,64]{1,3,2,0:T(8,128)(2,1)} %copy-done.22), kind=kOutput, calls=%fused_computation.30.clone.1 | convolution fusion | flops 836763648 | bytes 28098560 | tf_op jit(solution)/shard_map/while/body/eval_jaxpr/rhqk,rqhd->krhd/dot_general | solution.py:244
  547.6 17.0 %fusion.133 = bf16[12,1024,512]{1,2,0:T(8,128)(2,1)} fusion(f32[12,512,1024]{2,1,0:T(8,128)} %fusion.132, f32[12,1024]{1,0:T(8,128)S(1)} %bitcast.290, f32[12,1024]{1,0:T(8,128)S(1)} %bitcast.292, pred[1024,512]{0,1:T(8,128)(4,1)} %copy-done.6, bf16[512,12,64]{0,2,1:T(8,128)(2,1)S(1)} %bitcast.267, bf16[1,1024,12,64]{1,3,2,0:T(8,128)(2,1)} %copy-done.22), kind=kOutput, calls=%fused_computation.24.clone.1 | convolution fusion | flops 849346560 | bytes 40730624 | tf_op jit(solution)/shard_map/while/body/eval_jaxpr/rqhd,rkhd->rhqk/dot_general | solution.py:226
  564.6 9.4 fusion.135
  574.0 9.6 bitcast_add_fusion.8
  594.2 6.6 convolution_convert_fusion.2
  600.9 8.4 convolution_convert_fusion
  626.5 8.1 convolution_convert_fusion.1
  644.2 8.8 fusion.54
  653.0 20.8 %reduce-scatter.10.cloned.1.call-done = bf16[96,768]{1,0:T(8,128)(2,1)} async-done(((bf16[768,768]{1,0:T(8,128)(2,1)}), bf16[96,768]{1,0:T(8,128)(2,1)}) %reduce-scatter.10.cloned.1.call-update) | async-done | bytes 147472 | tf_op jit(solution)/shard_map/reduce_scatter | solution.py:91
  673.9 69.0 %reduce-scatter.14.cloned.1.call-done = bf16[144,768]{1,0:T(8,128)(2,1)} async-done(((bf16[1152,768]{1,0:T(8,128)(2,1)}), bf16[144,768]{1,0:T(8,128)(2,1)}) %reduce-scatter.14.cloned.1.call-update) | async-done | bytes 221200 | tf_op jit(solution)/shard_map/reduce_scatter | solution.py:91
  742.9 82.0 %reduce-scatter.12.cloned.1.call-done = bf16[96,2304]{1,0:T(8,128)(2,1)} async-done(((bf16[768,2304]{1,0:T(8,128)(2,1)}), bf16[96,2304]{1,0:T(8,128)(2,1)}) %reduce-scatter.12.cloned.1.call-update) | async-done | bytes 442384 | tf_op jit(solution)/shard_map/reduce_scatter | solution.py:91
  824.9 82.6 %reduce-scatter.8.cloned.1.call-done = bf16[96,2304]{1,0:T(8,128)(2,1)} async-done(((bf16[768,2304]{1,0:T(8,128)(2,1)}), bf16[96,2304]{1,0:T(8,128)(2,1)}) %reduce-scatter.8.cloned.1.call-update) | async-done | bytes 442384 | tf_op jit(solution)/shard_map/reduce_scatter | solution.py:91
  916.5 40.4 %all-reduce = (f32[768]{0:T(1024)}, f32[768]{0:T(1024)}) all-reduce(f32[768]{0:T(1024)S(1)} %get-tuple-element.272, f32[768]{0:T(1024)S(1)} %copy-done.40), channel_id=1, replica_groups=mesh['fsdp'=8,'rep'=2,'ctx'=2] {'fsdp','rep','ctx'}, use_global_device_ids=true, to_apply=%region_21.22 | all-reduce | flops 1536 | bytes 12288 | tf_op jit(solution)/shard_map/psum | solution.py:274
  (280 shorter events, 148.1 us)
Async XLA Ops:
  7.2 70.3 %all-gather.6.cloned.1.call-start = ((), (), s32[]{:S(2)}) async-start(), calls=%async_computation.5 | async-start | bytes 3981312 | tf_op jit(solution)/shard_map/all_gather | solution.py:76
  7.9 110.8 %all-gather.8.cloned.1.call-start = ((), (), s32[]{:S(2)}) async-start(), calls=%async_computation.6 | async-start | bytes 9437184 | tf_op jit(solution)/shard_map/all_gather | solution.py:175
  8.6 68.9 %copy-start.32 = (f32[768]{0:T(1024)}, f32[768]{0:T(1024)S(1)}, u32[]{:S(2)}) copy-start(f32[768]{0:T(1024)S(1)} %convert_element_type.174) | copy-start | bytes 9220
  10.4 73.3 %copy-start.1 = (bf16[1,1024,768]{1,2,0:T(8,128)(2,1)}, bf16[1,1024,768]{1,2,0:T(8,128)(2,1)S(1)}, u32[]{:S(2)}) copy-start(bf16[1,1024,768]{1,2,0:T(8,128)(2,1)S(1)} %copy.55) | copy-start | bytes 4718596
  11.0 72.7 %copy-start.28 = (f32[1024]{0:T(1024)}, f32[1024]{0:T(1024)S(1)}, u32[]{:S(2)}) copy-start(f32[1024]{0:T(1024)S(1)} %broadcast_multiply_fusion.5) | copy-start | bytes 12292
  11.5 72.3 %copy-start.34 = (f32[1024]{0:T(1024)}, f32[1024]{0:T(1024)S(1)}, u32[]{:S(2)}) copy-start(f32[1024]{0:T(1024)S(1)} %add_rsqrt_fusion.1) | copy-start | bytes 12292
  12.0 82.0 %copy-start.24 = (f32[1024,32]{0,1:T(8,128)}, f32[1024,32]{0,1:T(8,128)S(1)}, u32[]{:S(2)}) copy-start(f32[1024,32]{0,1:T(8,128)S(1)} %get-tuple-element.351) | copy-start | bytes 393220
  12.0 82.0 %copy-start.26 = (f32[1024,32]{0,1:T(8,128)}, f32[1024,32]{0,1:T(8,128)S(1)}, u32[]{:S(2)}) copy-start(f32[1024,32]{0,1:T(8,128)S(1)} %get-tuple-element.352) | copy-start | bytes 393220
  103.0 4.6 copy-start.17
  103.0 4.6 copy-start.18
  103.1 185.0 %all-gather.10.cloned.1.call-start = ((), (), s32[]{:S(2)}) async-start(), calls=%async_computation.7 | async-start | bytes 1327104 | tf_op jit(solution)/shard_map/all_gather | solution.py:76
  103.8 189.6 %all-gather.12.cloned.1.call-start = ((), (), s32[]{:S(2)}) async-start(), calls=%async_computation.8 | async-start | bytes 3981312 | tf_op jit(solution)/shard_map/all_gather | solution.py:76
  104.4 199.8 %all-gather.14.cloned.1.call-start = ((), (), s32[]{:S(2)}) async-start(), calls=%async_computation.9 | async-start | bytes 1990656 | tf_op jit(solution)/shard_map/all_gather | solution.py:76
  105.0 504.4 %reduce-scatter.6.cloned.1.call-start = ((), (), s32[]{:S(2)}) async-start(), calls=%async_computation.10 | async-start | bytes 9437184 | tf_op jit(solution)/shard_map/reduce_scatter | solution.py:258
  141.2 11.7 %copy-start.7 = (f32[1,12,1024,64]{2,3,1,0:T(8,128)S(1)}, f32[1,12,1024,64]{2,3,1,0:T(8,128)}, u32[]{:S(2)}) copy-start(f32[1,12,1024,64]{2,3,1,0:T(8,128)} %get-tuple-element.514) | copy-start | bytes 9437188 | tf_op jit(solution)/shard_map/while
  180.2 11.7 %copy-start.7 = (f32[1,12,1024,64]{2,3,1,0:T(8,128)S(1)}, f32[1,12,1024,64]{2,3,1,0:T(8,128)}, u32[]{:S(2)}) copy-start(f32[1,12,1024,64]{2,3,1,0:T(8,128)} %get-tuple-element.514) | copy-start | bytes 9437188 | tf_op jit(solution)/shard_map/while
  219.6 11.6 %copy-start.7 = (f32[1,12,1024,64]{2,3,1,0:T(8,128)S(1)}, f32[1,12,1024,64]{2,3,1,0:T(8,128)}, u32[]{:S(2)}) copy-start(f32[1,12,1024,64]{2,3,1,0:T(8,128)} %get-tuple-element.514) | copy-start | bytes 9437188 | tf_op jit(solution)/shard_map/while
  258.9 11.7 %copy-start.7 = (f32[1,12,1024,64]{2,3,1,0:T(8,128)S(1)}, f32[1,12,1024,64]{2,3,1,0:T(8,128)}, u32[]{:S(2)}) copy-start(f32[1,12,1024,64]{2,3,1,0:T(8,128)} %get-tuple-element.514) | copy-start | bytes 9437188 | tf_op jit(solution)/shard_map/while
  291.3 26.6 %copy-start.30 = (f32[1024]{0:T(1024)}, f32[1024]{0:T(1024)S(1)}, u32[]{:S(2)}) copy-start(f32[1024]{0:T(1024)S(1)} %broadcast_multiply_fusion.4) | copy-start | bytes 12292
  293.4 24.6 %copy-start.38 = (f32[1024]{0:T(1024)}, f32[1024]{0:T(1024)S(1)}, u32[]{:S(2)}) copy-start(f32[1024]{0:T(1024)S(1)} %add_rsqrt_fusion) | copy-start | bytes 12292
  293.4 10.8 %copy-start.20 = (bf16[1,1024,768]{2,1,0:T(8,128)(2,1)S(1)}, bf16[1,1024,768]{2,1,0:T(8,128)(2,1)}, u32[]{:S(2)}) copy-start(bf16[1,1024,768]{2,1,0:T(8,128)(2,1)} %param.14) | copy-start | bytes 4718596
  304.2 8.9 copy-start.11
  304.2 8.9 copy-start.43
  313.1 4.9 copy-start.45
  313.1 4.9 copy-start.46
  313.1 4.9 copy-start.15
  324.9 11.8 %copy-start.6 = (pred[1024,512]{0,1:T(8,128)(4,1)}, pred[1024,512]{0,1:T(8,128)(4,1)S(1)}, u32[]{:S(2)}) copy-start(pred[1024,512]{0,1:T(8,128)(4,1)S(1)} %broadcast_compare_fusion.5) | copy-start | bytes 1572868 | tf_op jit(solution)/shard_map/while
  375.6 8.7 copy-start.4
  375.6 8.7 copy-start.5
  390.5 11.8 %copy-start.6 = (pred[1024,512]{0,1:T(8,128)(4,1)}, pred[1024,512]{0,1:T(8,128)(4,1)S(1)}, u32[]{:S(2)}) copy-start(pred[1024,512]{0,1:T(8,128)(4,1)S(1)} %broadcast_compare_fusion.5) | copy-start | bytes 1572868 | tf_op jit(solution)/shard_map/while
  441.1 9.6 copy-start.4
  441.1 9.6 copy-start.5
  456.9 11.8 %copy-start.6 = (pred[1024,512]{0,1:T(8,128)(4,1)}, pred[1024,512]{0,1:T(8,128)(4,1)S(1)}, u32[]{:S(2)}) copy-start(pred[1024,512]{0,1:T(8,128)(4,1)S(1)} %broadcast_compare_fusion.5) | copy-start | bytes 1572868 | tf_op jit(solution)/shard_map/while
  507.6 9.6 copy-start.4
  507.6 9.6 copy-start.5
  523.4 11.8 %copy-start.6 = (pred[1024,512]{0,1:T(8,128)(4,1)}, pred[1024,512]{0,1:T(8,128)(4,1)S(1)}, u32[]{:S(2)}) copy-start(pred[1024,512]{0,1:T(8,128)(4,1)S(1)} %broadcast_compare_fusion.5) | copy-start | bytes 1572868 | tf_op jit(solution)/shard_map/while
  574.0 9.6 copy-start.4
  574.0 9.6 copy-start.5
  588.3 85.5 %reduce-scatter.10.cloned.1.call-start = ((), (), s32[]{:S(2)}) async-start(), calls=%async_computation.12 | async-start | bytes 1327104 | tf_op jit(solution)/shard_map/reduce_scatter | solution.py:91
  594.1 148.8 %reduce-scatter.14.cloned.1.call-start = ((), (), s32[]{:S(2)}) async-start(), calls=%async_computation.14 | async-start | bytes 1990656 | tf_op jit(solution)/shard_map/reduce_scatter | solution.py:91
  594.1 6.7 copy-start.12
  594.1 6.7 copy-start.31
  594.1 6.7 copy-start.37
  594.2 6.7 copy-start.39
  600.8 224.1 %reduce-scatter.12.cloned.1.call-start = ((), (), s32[]{:S(2)}) async-start(), calls=%async_computation.13 | async-start | bytes 3981312 | tf_op jit(solution)/shard_map/reduce_scatter | solution.py:91
  609.3 298.2 %reduce-scatter.8.cloned.1.call-start = ((), (), s32[]{:S(2)}) async-start(), calls=%async_computation.11 | async-start | bytes 3981312 | tf_op jit(solution)/shard_map/reduce_scatter | solution.py:91
  613.8 3.7 copy-start.27
  634.6 322.3 %all-reduce.4.cloned.1.call-start = ((), (), s32[]{:S(2)}) async-start(), calls=%async_computation.15 | async-start | bytes 2506752 | tf_op jit(solution)/shard_map/psum | solution.py:99
  (31 other events, 75.5 us)
Sparse Core Ops, SparseCore 0:
  10.2 67.3 all-gather.5
  103.2 15.4 all-gather.7
  120.9 42.2 all-gather.9
  165.3 63.2 all-gather.11
  230.6 44.6 all-gather.13
  588.5 15.1 reduce-scatter.5
  607.1 66.7 reduce-scatter.9
  677.3 65.5 reduce-scatter.13
  746.5 78.2 reduce-scatter.11
  828.4 79.0 reduce-scatter.7
  910.1 39.0 all-reduce.3
where the time goes:
time: 979 us; the launch traced here: 971 us
  matrix products  401 us (41%)
  waiting for transfers between devices  333 us (34%)
  other arithmetic  89.3 us (9%)
  local copies, waits for them, and re-layouts  84.5 us (9%)
  blocking collectives  40.4 us (4%)
  between operations  14.9 us (2%)
    reduce_scatter x4, waiting for transfers between devices, weight_grad(): lax.psum_scatter(lax.dot_general(activations, gradient, (((0,), (0,)), ((...  254 us
    dot_general x8, matrix products, score_block(): jnp.einsum('rqhd,rkhd->rhqk', query_rows, key_rows, preferred_element_typ...  83.2 us
    dot_general x4, matrix products, block_parts(): jnp.einsum('rqhd,rkhd->rhqk', d_att, value_block, preferred_element_type=...  68 us
    all_gather x4, waiting for transfers between devices, project(): lax.all_gather(weight, 'fsdp', axis=0, tiled=True)  65.5 us
    dot_general x4, matrix products, both_step(): jnp.einsum('rhqk,rqhd->krhd', probs_half, d_att, preferred_element_type=j...  49.6 us
    dot_general x4, matrix products, step_block(): jnp.einsum('rhqk,rkhd->rhqd', weights.astype(jnp.bfloat16), value_block,...  47.8 us
    reduce_sum x4, other arithmetic, step_block(): new_sum = run_sum * factor + jnp.sum(weights, axis=-1)  46.6 us
    psum x1, blocking collectives, per_device(): lax.psum((local_attn_gain, local_mlp_gain), ('fsdp', 'rep', 'ctx'))  40.4 us
  transfers between devices with their start and end apart: 11, of which 6 were waited for; matrix products, arithmetic and copies ran while one was open for 26% of the time, Pallas kernels for 0%

commit v1 on v0

v1 whole, which is shorter than its diff:
```python
import functools

import jax
import jax.numpy as jnp
from jax import lax
from jax.experimental import pallas as pl
from jax.experimental.pallas import tpu as pltpu
from jax.sharding import PartitionSpec as P

HD = 64
PAIR = 2 * HD

norm_eps = 1e-05
rope_base = 160000.0
masked_score = -1e30
QB = 256
KB = 256
bf16 = jnp.bfloat16
f32 = jnp.float32
NT = (((1,), (1,)), ((), ()))


def params(count):
    return pltpu.CompilerParams(
        dimension_semantics=("arbitrary",) * count, vmem_limit_bytes=56 * 1024 * 1024
    )


def layer_norm(values):
    center = values - jnp.mean(values, axis=-1, keepdims=True)
    inverse = lax.rsqrt(jnp.mean(center * center, axis=-1, keepdims=True) + norm_eps)
    return (center * inverse, inverse)


def norm_back(grad_normed, normed, inverse):
    mean_grad = jnp.mean(grad_normed, axis=-1, keepdims=True)
    mean_cross = jnp.mean(grad_normed * normed, axis=-1, keepdims=True)
    return (grad_normed - mean_grad - normed * mean_cross) * inverse


def gelu_pair(values):
    cumulative = 0.5 * (1.0 + lax.erf(values * 0.7071067811865476))
    density = jnp.exp(-0.5 * values * values) * 0.3989422804014327
    return (values * cumulative, cumulative + values * density)


def doc_tables(lengths, positions):
    doc_ends = jnp.cumsum(lengths)
    before = (doc_ends[None, :] <= positions[:, None]).astype(jnp.int32)
    segment = jnp.sum(before, axis=1)
    begins = jnp.sum(before * lengths[None, :], axis=1)
    return (segment, positions - begins)


def rope_lanes(offsets):
    lane = jnp.arange(PAIR, dtype=jnp.int32) % HD
    frequency = rope_base ** (-((lane % (HD // 2)).astype(f32) * (2.0 / HD)))
    angles = offsets.astype(f32)[:, None] * frequency
    sign = jnp.where(lane < HD // 2, -1.0, 1.0).astype(f32)
    return (jnp.cos(angles), jnp.sin(angles) * sign)


def swap_halves(values):
    lane = lax.broadcasted_iota(jnp.int32, values.shape, 1)
    front = (lane % HD) < HD // 2
    return jnp.where(
        front,
        pltpu.roll(values, PAIR - HD // 2, 1),
        pltpu.roll(values, HD // 2, 1),
    )


def qkv_kernel(x_ref, gain_ref, cos_ref, sin_ref, w_ref, act_ref, q_ref, kv_ref):
    width = x_ref.shape[1]
    normed, _ = layer_norm(x_ref[...].astype(f32))
    act = (normed * gain_ref[...].astype(f32)).astype(bf16)
    act_ref[...] = act
    cosine, sine = cos_ref[...], sin_ref[...]
    for start in range(0, 3 * width, 2 * PAIR):
        part = jnp.dot(act, w_ref[:, start : start + 2 * PAIR], preferred_element_type=f32)
        for half in range(2):
            at = start + half * PAIR
            piece = part[:, half * PAIR : (half + 1) * PAIR]
            if at < 2 * width:
                piece = piece * cosine + swap_halves(piece) * sine
            if at < width:
                q_ref[:, at : at + PAIR] = piece.astype(bf16)
            else:
                kv_ref[:, at - width : at - width + PAIR] = piece.astype(bf16)


def qkv_call(inputs, gain, cosine, sine, weight):
    count, width = inputs.shape
    rows = min(256, count)
    row = lambda n: pl.BlockSpec((rows, n), lambda i: (i, 0))
    whole = lambda a: pl.BlockSpec(a.shape, lambda i: (0, 0))
    return pl.pallas_call(
        qkv_kernel,
        grid=(count // rows,),
        in_specs=[row(width), whole(gain), row(PAIR), row(PAIR), whole(weight)],
        out_specs=[row(width), row(width), row(2 * width)],
        out_shape=[
            jax.ShapeDtypeStruct((count, width), bf16),
            jax.ShapeDtypeStruct((count, width), bf16),
            jax.ShapeDtypeStruct((count, 2 * width), bf16),
        ],
        compiler_params=params(1),
        cost_estimate=pl.CostEstimate(
            flops=6 * count * width * width, bytes_accessed=12 * 1024 * 1024, transcendentals=0
        ),
    )(inputs, gain, cosine, sine, weight)


def split_heads(values, mark):
    lane = lax.broadcasted_iota(jnp.int32, values.shape, 1)
    zero = jnp.zeros_like(values)
    front, back = jnp.where(lane < HD, values, zero), jnp.where(lane < HD, zero, values)
    if mark is None:
        return front, back
    return jnp.concatenate([front, mark], axis=1), jnp.concatenate([back, mark], axis=1)


def fwd_kernel(step, lo_ref, hi_ref, q_ref, k_ref, v_ref, qm_ref, km_ref, o_ref, lse_ref, vt_ref):
    r, block = pl.program_id(0), pl.program_id(2)
    scale = HD ** (-0.5)

    @pl.when(block == 0)
    def _():
        for i in range(vt_ref.shape[0]):
            vt_ref[i] = v_ref[0, i * step : (i + 1) * step, :].T

    queries = split_heads((q_ref[0].astype(f32) * scale).astype(bf16), qm_ref[0])
    count = q_ref.shape[1]

    def body(index, carry):
        rows = pl.ds(pl.multiple_of(index * step, step), step)
        keys = jnp.concatenate([k_ref[0, rows, :], km_ref[0, rows, :]], axis=1)
        turned = vt_ref[index]
        result = []
        for h in range(2):
            run_max, run_sum, accum = carry[h]
            scores = lax.dot_general(keys, queries[h], NT, preferred_element_type=f32)
            new_max = jnp.maximum(run_max, jnp.max(scores, axis=0, keepdims=True))
            weights = jnp.exp(scores - new_max)
            factor = jnp.exp(run_max - new_max)
            new_sum = run_sum * factor + jnp.sum(weights, axis=0, keepdims=True)
            new_acc = accum * factor + jnp.dot(
                turned[h * HD : (h + 1) * HD], weights.astype(bf16), preferred_element_type=f32
            )
            result.append((new_max, new_sum, new_acc))
        return tuple(result)

    one = (
        jnp.full((1, count), masked_score, f32),
        jnp.zeros((1, count), f32),
        jnp.zeros((HD, count), f32),
    )
    state = lax.fori_loop(lo_ref[r, block], hi_ref[r, block], body, (one, one))
    outs = []
    for h in range(2):
        run_max, run_sum, accum = state[h]
        lse_ref[0, 0, h : h + 1, :] = run_max + jnp.log(run_sum)
        outs.append(accum / run_sum)
    o_ref[0] = jnp.concatenate(outs, axis=0).T.astype(bf16)


def fwd_call(lo, hi, query, kv, qmark, kmark, step):
    rows_here, count, width = query.shape
    length = kv.shape[1]
    pairs = width // PAIR
    qb = count // lo.shape[1]
    qspec = pl.BlockSpec((1, qb, PAIR), lambda r, h, i, *_: (r, i, h))
    return pl.pallas_call(
        functools.partial(fwd_kernel, step),
        grid_spec=pltpu.PrefetchScalarGridSpec(
            num_scalar_prefetch=2,
            grid=(rows_here, pairs, count // qb),
            in_specs=[
                qspec,
                pl.BlockSpec((1, length, PAIR), lambda r, h, i, *_: (r, 0, h)),
                pl.BlockSpec((1, length, PAIR), lambda r, h, i, *_: (r, 0, h + pairs)),
                pl.BlockSpec((1, qb, PAIR), lambda r, h, i, *_: (r, i, 0)),
                pl.BlockSpec((1, length, PAIR), lambda r, h, i, *_: (r, 0, 0)),
            ],
            out_specs=[
                qspec,
                pl.BlockSpec((1, 1, 2, qb), lambda r, h, i, *_: (r, h, 0, i)),
            ],
            scratch_shapes=[pltpu.VMEM((length // step, PAIR, step), bf16)],
        ),
        out_shape=[
            jax.ShapeDtypeStruct(query.shape, bf16),
            jax.ShapeDtypeStruct((rows_here, pairs, 2, count), f32),
        ],
        compiler_params=params(3),
        cost_estimate=pl.CostEstimate(
            flops=rows_here * 8 * count * length * width,
            bytes_accessed=16 * 1024 * 1024,
            transcendentals=0,
        ),
    )(lo, hi, query, kv, kv, qmark, kmark)


def bwd_kernel(
    step, lo_ref, hi_ref, q_ref, k_ref, v_ref, qm_ref, km_ref, do_ref, o_ref, lse_ref,
    cos_ref, sin_ref, dq_ref, dkv_ref, kt_ref, dk_acc, dv_acc,
):
    r, block = pl.program_id(0), pl.program_id(2)
    scale = HD ** (-0.5)

    @pl.when(block == 0)
    def _():
        for i in range(kt_ref.shape[0]):
            kt_ref[i] = k_ref[0, i * step : (i + 1) * step, :].T
        dk_acc[...] = jnp.zeros_like(dk_acc)
        dv_acc[...] = jnp.zeros_like(dv_acc)

    count = q_ref.shape[1]
    scaled = (q_ref[0].astype(f32) * scale).astype(bf16)
    queries = split_heads(scaled, qm_ref[0])
    query_rows = jnp.concatenate(split_heads(scaled, None), axis=0)
    grads = split_heads(do_ref[0], None)
    grad_rows = jnp.concatenate(grads, axis=0)
    products = (do_ref[0].astype(f32) * o_ref[0].astype(f32)).T
    deltas = [jnp.sum(products[h * HD : (h + 1) * HD], axis=0, keepdims=True) for h in range(2)]
    totals = [lse_ref[0, 0, h : h + 1, :] for h in range(2)]

    def body(index, carry):
        rows = pl.ds(pl.multiple_of(index * step, step), step)
        keys = jnp.concatenate([k_ref[0, rows, :], km_ref[0, rows, :]], axis=1)
        values = v_ref[0, rows, :]
        turned = kt_ref[index]
        result, probs_all, ds_all = [], [], []
        for h in range(2):
            scores = lax.dot_general(keys, queries[h], NT, preferred_element_type=f32)
            probs = jnp.exp(scores - totals[h])
            d_probs = lax.dot_general(values, grads[h], NT, preferred_element_type=f32)
            d_scores = (probs * (d_probs - deltas[h])).astype(bf16)
            result.append(
                carry[h]
                + jnp.dot(turned[h * HD : (h + 1) * HD], d_scores, preferred_element_type=f32)
            )
            probs_all.append(probs.astype(bf16))
            ds_all.append(d_scores)
        dv_acc[rows, :] += jnp.dot(
            jnp.concatenate(probs_all, axis=1), grad_rows, preferred_element_type=f32
        )
        dk_acc[rows, :] += jnp.dot(
            jnp.concatenate(ds_all, axis=1), query_rows, preferred_element_type=f32
        )
        return tuple(result)

    zero = jnp.zeros((HD, count), f32)
    state = lax.fori_loop(lo_ref[r, block], hi_ref[r, block], body, (zero, zero))
    d_query = jnp.concatenate(state, axis=0).T * scale
    d_query = d_query * cos_ref[0] - swap_halves(d_query) * sin_ref[0]
    dq_ref[0] = d_query.astype(bf16)

    @pl.when(block == pl.num_programs(2) - 1)
    def _():
        dkv_ref[0, 0] = dk_acc[...].astype(bf16)
        dkv_ref[1, 0] = dv_acc[...].astype(bf16)


def bwd_call(lo, hi, query, kv, qmark, kmark, d_att, att, lse, cosine, sine, step):
    rows_here, count, width = query.shape
    length = kv.shape[1]
    pairs = width // PAIR
    qb = count // lo.shape[1]
    qspec = pl.BlockSpec((1, qb, PAIR), lambda r, h, i, *_: (r, i, h))
    tspec = pl.BlockSpec((1, qb, PAIR), lambda r, h, i, *_: (r, i, 0))
    return pl.pallas_call(
        functools.partial(bwd_kernel, step),
        grid_spec=pltpu.PrefetchScalarGridSpec(
            num_scalar_prefetch=2,
            grid=(rows_here, pairs, count // qb),
            in_specs=[
                qspec,
                pl.BlockSpec((1, length, PAIR), lambda r, h, i, *_: (r, 0, h)),
                pl.BlockSpec((1, length, PAIR), lambda r, h, i, *_: (r, 0, h + pairs)),
                tspec,
                pl.BlockSpec((1, length, PAIR), lambda r, h, i, *_: (r, 0, 0)),
                qspec,
                qspec,
                pl.BlockSpec((1, 1, 2, qb), lambda r, h, i, *_: (r, h, 0, i)),
                tspec,
                tspec,
            ],
            out_specs=[
                qspec,
                pl.BlockSpec((2, 1, length, PAIR), lambda r, h, i, *_: (0, r, 0, h)),
            ],
            scratch_shapes=[
                pltpu.VMEM((length // step, PAIR, step), bf16),
                pltpu.VMEM((length, PAIR), f32),
                pltpu.VMEM((length, PAIR), f32),
            ],
        ),
        out_shape=[
            jax.ShapeDtypeStruct(query.shape, bf16),
            jax.ShapeDtypeStruct((2, rows_here, length, width), bf16),
        ],
        compiler_params=params(3),
        cost_estimate=pl.CostEstimate(
            flops=rows_here * 20 * count * length * width,
            bytes_accessed=24 * 1024 * 1024,
            transcendentals=0,
        ),
    )(lo, hi, query, kv, kv, qmark, kmark, d_att, att, lse, cosine, sine)


def join_kernel(parts, *refs):
    dq_ref, cos_ref, sin_ref = refs[:3]
    sides, out_ref = refs[3:-1], refs[-1]
    width = dq_ref.shape[1]
    out_ref[:, :width] = dq_ref[...]
    for at in range(0, width, PAIR):
        lanes = slice(at, at + PAIR)
        d_key = sum(s[0, :, lanes].astype(f32) for s in sides)
        d_key = d_key * cos_ref[...] - swap_halves(d_key) * sin_ref[...]
        out_ref[:, width + at : width + at + PAIR] = d_key.astype(bf16)
        d_value = sum(s[1, :, lanes].astype(f32) for s in sides)
        out_ref[:, 2 * width + at : 2 * width + at + PAIR] = d_value.astype(bf16)


def join_call(dq, cosine, sine, sides):
    count, width = dq.shape
    rows = min(256, count)
    row = lambda n: pl.BlockSpec((rows, n), lambda i: (i, 0))
    return pl.pallas_call(
        functools.partial(join_kernel, len(sides)),
        grid=(count // rows,),
        in_specs=[row(width), row(PAIR), row(PAIR)]
        + [pl.BlockSpec((2, rows, width), lambda i: (0, i, 0))] * len(sides),
        out_specs=row(3 * width),
        out_shape=jax.ShapeDtypeStruct((count, 3 * width), bf16),
        compiler_params=params(1),
        cost_estimate=pl.CostEstimate(
            flops=count * width * 10, bytes_accessed=12 * 1024 * 1024, transcendentals=0
        ),
    )(dq, cosine, sine, *sides)


def token_grad(activations, gradient):
    return lax.dot_general(
        activations, gradient, (((0,), (0,)), ((), ())), preferred_element_type=f32
    ).astype(bf16)


def matmul_back(gradient, weight):
    return lax.dot_general(gradient, weight, NT, preferred_element_type=f32)


def per_device(
    sizes,
    tokens,
    cotangent,
    doc_lengths,
    attn_gain,
    qkv_weight,
    out_weight,
    mlp_gain,
    in_weight,
    down_weight,
):
    rows_here, block_len, width = tokens.shape
    ctx_size = sizes["ctx"]
    length = block_len * ctx_size
    flat_count = rows_here * block_len
    hidden = down_weight.shape[0] * sizes["fsdp"]
    docs = doc_lengths.shape[1]

    def pair_sum(value, axis):
        if sizes[axis] == 2:
            other = lax.ppermute(value, axis, [(0, 1), (1, 0)])
            return value.astype(f32) + other.astype(f32)
        return lax.psum(value, axis).astype(f32)

    def gather(weight):
        return lax.all_gather(weight, "fsdp", axis=0, tiled=True)

    def scatter(grad):
        return lax.psum_scatter(grad, "fsdp", scatter_dimension=0, tiled=True)

    def replica_sum(shard):
        return pair_sum(pair_sum(shard, "ctx").astype(bf16), "rep")

    ctx_index = lax.axis_index("ctx")
    first_pos = ctx_index * block_len
    local_pos = first_pos + jnp.arange(block_len, dtype=jnp.int32)
    all_pos = jnp.arange(length, dtype=jnp.int32)
    seg_all, _ = jax.vmap(doc_tables, in_axes=(0, None))(doc_lengths, all_pos)
    seg_query, offsets = jax.vmap(doc_tables, in_axes=(0, None))(doc_lengths, local_pos)
    cosine, sine = rope_lanes(offsets.reshape(flat_count))
    lane = jnp.arange(PAIR, dtype=jnp.int32)
    qmark = (seg_query[:, :, None] == lane).astype(bf16)
    kmark = jnp.where(
        (seg_all[:, :, None] != lane) & (lane < docs), masked_score, 0.0
    ).astype(bf16)
    qb = min(QB, block_len)
    step = min(KB, length)
    ends = jnp.cumsum(doc_lengths, axis=1)
    low_pos = first_pos + jnp.arange(block_len // qb, dtype=jnp.int32) * qb
    high_pos = low_pos + qb - 1
    past = lambda pos: ends[:, None, :] <= pos[None, :, None]
    lo = jnp.max(jnp.where(past(low_pos), ends[:, None, :], 0), axis=-1) // step
    hi = jnp.min(jnp.where(past(high_pos), length, ends[:, None, :]), axis=-1)
    hi = (hi + step - 1) // step

    inputs_half = tokens.reshape(flat_count, width)
    full_qkv = gather(qkv_weight)
    act_attn, query, kv_local = qkv_call(
        inputs_half, attn_gain.reshape(1, width), cosine, sine, full_qkv
    )
    shaped = (rows_here, block_len, width)
    query = query.reshape(shaped)
    kv_local = kv_local.reshape(rows_here, block_len, 2 * width)
    if ctx_size == 2:
        kv_other = lax.ppermute(kv_local, "ctx", [(0, 1), (1, 0)])
        first = ctx_index == 0
        kv_all = jnp.concatenate(
            [jnp.where(first, kv_local, kv_other), jnp.where(first, kv_other, kv_local)], axis=1
        )
    else:
        kv_all = lax.all_gather(kv_local, "ctx", axis=1, tiled=True)
    full_out, full_in, full_down = gather(out_weight), gather(in_weight), gather(down_weight)
    attended, lse = fwd_call(lo, hi, query, kv_all, qmark, kmark, step)
    att_flat = attended.reshape(flat_count, width)
    inputs = inputs_half.astype(f32)
    residual = inputs + jnp.dot(att_flat, full_out, preferred_element_type=f32)
    normed_mlp, inverse_mlp = layer_norm(residual)
    act_mlp = (normed_mlp * mlp_gain.astype(f32)).astype(bf16)
    up_all = jnp.dot(act_mlp, full_in, preferred_element_type=f32)
    inner, gate = (up_all[:, :hidden], up_all[:, hidden:])
    gelu_value, gelu_slope = gelu_pair(inner)
    mixed = (gelu_value * gate).astype(bf16)
    output = (residual + jnp.dot(mixed, full_down, preferred_element_type=f32)).astype(bf16)
    cot_flat = cotangent.reshape(flat_count, width)
    d_mixed = matmul_back(cot_flat, full_down)
    d_up = jnp.concatenate([d_mixed * gate * gelu_slope, d_mixed * gelu_value], axis=-1).astype(
        bf16
    )
    local_down = token_grad(mixed, cot_flat)
    local_in = token_grad(act_mlp, d_up)
    d_act_mlp = matmul_back(d_up, full_in)
    local_mlp_gain = jnp.sum(d_act_mlp * normed_mlp, axis=0)
    d_residual = cot_flat.astype(f32) + norm_back(
        d_act_mlp * mlp_gain.astype(f32), normed_mlp, inverse_mlp
    )
    d_res_half = d_residual.astype(bf16)
    local_out = token_grad(att_flat, d_res_half)
    d_att = matmul_back(d_res_half, full_out).astype(bf16).reshape(shaped)
    early_in, early_out, early_down = scatter(local_in), scatter(local_out), scatter(local_down)
    grad_in = replica_sum(early_in)
    grad_out = replica_sum(early_out)
    grad_down = replica_sum(early_down)
    d_query, pair_terms = bwd_call(
        lo, hi, query, kv_all, qmark, kmark, d_att, attended, lse,
        cosine.reshape(rows_here, block_len, PAIR), sine.reshape(rows_here, block_len, PAIR), step,
    )
    if ctx_size == 2:
        mine = lax.dynamic_slice_in_dim(pair_terms, first_pos, block_len, 2)
        theirs = lax.dynamic_slice_in_dim(pair_terms, block_len - first_pos, block_len, 2)
        sides = [mine, lax.ppermute(theirs, "ctx", [(0, 1), (1, 0)])]
    else:
        sides = [lax.psum_scatter(pair_terms, "ctx", scatter_dimension=2, tiled=True)]
    sides = [s.reshape(2, flat_count, width) for s in sides]
    d_qkv = join_call(d_query.reshape(flat_count, width), cosine, sine, sides)
    local_qkv = token_grad(act_attn, d_qkv)
    grad_qkv = replica_sum(scatter(local_qkv))
    d_act_attn = matmul_back(d_qkv, full_qkv)
    normed_attn, inverse_attn = layer_norm(inputs)
    local_attn_gain = jnp.sum(d_act_attn * normed_attn, axis=0)
    input_grad = d_residual + norm_back(
        d_act_attn * attn_gain.astype(f32), normed_attn, inverse_attn
    )
    gains = lax.psum(jnp.stack([local_attn_gain, local_mlp_gain]), ("fsdp", "rep", "ctx"))
    grad_attn_gain, grad_mlp_gain = gains[0], gains[1]
    return (
        output.reshape(shaped),
        input_grad.reshape(shaped),
        grad_attn_gain,
        grad_qkv,
        grad_out,
        grad_mlp_gain,
        grad_in,
        grad_down,
    )


def solution(mesh):
    return jax.shard_map(
        functools.partial(per_device, dict(mesh.shape)),
        mesh=mesh,
        in_specs=(
            P(("fsdp", "rep"), "ctx", None),
            P(("fsdp", "rep"), "ctx", None),
            P(("fsdp", "rep"), None),
            P(),
            P("fsdp", None),
            P("fsdp", None),
            P(),
            P("fsdp", None),
            P("fsdp", None),
        ),
        out_specs=(
            P(("fsdp", "rep"), "ctx", None),
            P(("fsdp", "rep"), "ctx", None),
            P(),
            P("fsdp", None),
            P("fsdp", None),
            P(),
            P("fsdp", None),
            P("fsdp", None),
        ),
        check_vma=False,
    )
```

time: 979 us -> 585 us (0.60)
  matrix products: 401 us -> 68.8 us
  Pallas kernels: 0 us -> 207 us
  waiting for transfers between devices: 333 us -> 197 us
  local copies, waits for them, and re-layouts: 84.5 us -> 14.7 us
  other arithmetic: 89.3 us -> 30.4 us
    dot_general x40 -> x11, matrix products: 401 us -> 68.8 us  [the longest x4 24.4 us: token_grad(): lax.dot_general(activations, gradient, (((0,), (0,)), ((), ())), preferre...]
    pallas_call x0 -> x4, Pallas kernels: none -> 207 us  [the longest x1 98.2 us: bwd_call(): pl.pallas_call(functools.partial(bwd_kernel, step), grid_spec=pltpu.Prefe...]
    reduce_scatter x5 -> x4, waiting for transfers between devices: 254 us -> 83.7 us  [scatter(): return lax.psum_scatter(grad, 'fsdp', scatter_dimension=0, tiled=True)]
    reduce_sum x6 -> x0, other arithmetic: 47.4 us -> none  [the longest x4 46.6 us: step_block(): new_sum = run_sum * factor + jnp.sum(weights, axis=-1)]
    ppermute x0 -> x10, waiting for transfers between devices: none -> 24.1 us  [the longest x8 19.1 us: pair_sum(): other = lax.ppermute(value, axis, [(0, 1), (1, 0)])]
    slice x11 -> x1, local copies, waits for them, and re-layouts: 21.7 us -> 0.61 us  [per_device(): grad_attn_gain, grad_mlp_gain = (gains[0], gains[1])]
    unnamed x85 -> x34, local copies, waits for them, and re-layouts: 23.8 us -> 5.28 us
    dynamic_update_slice x8 -> x0, local copies, waits for them, and re-layouts: 17.6 us -> none  [per_device(): lax.scan(both_step, zero_query, jnp.arange(key_count, dtype=jnp.int32))]
  transfers between devices with their start and end apart: 11 -> 18, of which waited for: 6 -> 9; matrix products, arithmetic and copies ran while one was open for 26% -> 16% of each run, Pallas kernels for 0% -> 36%
where the time goes in v1:
time: 585 us; the launch traced here: 580 us
  Pallas kernels  207 us (35%)
  waiting for transfers between devices  197 us (34%)
  matrix products  68.8 us (12%)
  blocking collectives  42.1 us (7%)
  other arithmetic  30.4 us (5%)
  between operations  14.9 us (3%)
  local copies, waits for them, and re-layouts  14.7 us (3%)
    pallas_call x1, Pallas kernels, bwd_call(): pl.pallas_call(functools.partial(bwd_kernel, step), grid_spec=pltpu.Prefe...  98.2 us
    pallas_call x1, Pallas kernels, fwd_call(): pl.pallas_call(functools.partial(fwd_kernel, step), grid_spec=pltpu.Prefe...  93 us
    all_gather x4, waiting for transfers between devices, gather(): return lax.all_gather(weight, 'fsdp', axis=0, tiled=True)  87.2 us
    reduce_scatter x4, waiting for transfers between devices, scatter(): return lax.psum_scatter(grad, 'fsdp', scatter_dimension=0, tiled=True)  83.7 us
    psum x1, blocking collectives, per_device(): lax.psum(jnp.stack([local_attn_gain, local_mlp_gain]), ('fsdp', 'rep', 'c...  42.1 us
    dot_general x4, matrix products, token_grad(): lax.dot_general(activations, gradient, (((0,), (0,)), ((), ())), preferre...  24.4 us
    dot_general x4, matrix products, matmul_back(): return lax.dot_general(gradient, weight, NT, preferred_element_type=f32)  23.6 us
    ppermute x8, waiting for transfers between devices, pair_sum(): other = lax.ppermute(value, axis, [(0, 1), (1, 0)])  19.1 us
  transfers between devices with their start and end apart: 18, of which 9 were waited for; matrix products, arithmetic and copies ran while one was open for 16% of the time, Pallas kernels for 36%

profile of v1, /device:TPU:0, one launch (start us, length us, event | category | flops | bytes accessed | tf_op | source)
XLA Modules:
  0.0 580.3 jit_solution(1645341804590146347)
XLA Ops:
  9.4 1.3 reshape.870.gain_ref
  10.7 0.8 reduce-window.7
  12.3 3.1 fusion.33
  15.4 62.1 %all-gather.5.cloned.1.call-done.w_ref = bf16[768,2304]{1,0:T(8,128)(2,1)} async-done(((bf16[96,2304]{1,0:T(8,128)(2,1)}), bf16[768,2304]{1,0:T(8,128)(2,1)}) %all-gather.5.cloned.1.call-update) | async-done | bytes 3538960 | tf_op jit(solution)/shard_map/all_gather | solution.py:380
  77.5 8.8 %shard_map.152 = (bf16[1024,768]{1,0:T(8,128)(2,1)}, bf16[1024,768]{1,0:T(8,128)(2,1)}, bf16[1024,1536]{1,0:T(8,128)(2,1)}) custom-call(bf16[1024,768]{1,0:T(8,128)(2,1)} %bitcast.70, bf16[1,768]{1,0:T(2,128)(2,1)} %reshape.870.gain_ref, f32[1024,128]{1,0:T(8,128)} %get-tuple-element.42.cos_ref.refs_1_, f32[1024,128]{1,0:T(8,128)} %get-tuple-element.41.sin_ref.refs_2_, ...), custom_call_target="tpu_custom_call" | custom-call | flops 3623878656 | bytes 12582912 | tf_op jit(solution)/shard_map/pallas_call | solution.py:97
  87.3 0.9 fusion.35.qm_ref
  88.2 1.1 select_convert_fusion.km_ref
  89.4 2.8 collective-permute-done
  92.2 2.3 broadcast_select_fusion.1
  94.5 3.1 pad_maximum_fusion.k_ref.v_ref
  97.6 93.0 %shard_map.153 = (bf16[1,1024,768]{2,1,0:T(8,128)(2,1)}, f32[1,6,2,1024]{3,2,1,0:T(2,128)}) custom-call(s32[1,4]{1,0:T(1,128)} %get-tuple-element.50.lo_ref, s32[1,4]{1,0:T(1,128)} %get-tuple-element.49.hi_ref, bf16[1,1024,768]{2,1,0:T(8,128)(2,1)} %bitcast.81, bf16[1,2048,1536]{2,1,0:T(8,128)(2,1)} %pad_maximum_fusion.k_ref.v_ref, ...), custom_call_target="tpu_custom_call" | custom-call | flops 12884901888 | bytes 16777216 | tf_op jit(solution)/shard_map/pallas_call | solution.py:173
  190.7 3.3 fusion.46
  194.0 1.6 copy-done.1
  196.2 10.7 %fusion.45 = f32[1024,2304]{1,0:T(8,128)} fusion(bf16[768,2304]{1,0:T(8,128)(2,1)} %all-gather.9.cloned.1.call-done, f32[1024,768]{1,0:T(8,128)} %copy-done.1, f32[768]{0:T(1024)S(1)} %convert_element_type.152, f32[1024]{0:T(1024)S(1)} %add_rsqrt_fusion.1, f32[1024]{0:T(1024)S(1)} %broadcast_multiply_fusion.5), kind=kOutput, calls=%fused_computation.122 | convolution fusion | flops 3627024384 | bytes 16133120 | tf_op jit(solution)/shard_map/dot_general | solution.py:433
  206.9 25.0 %all-gather.11.cloned.1.call-done = bf16[1152,768]{1,0:T(8,128)(2,1)} async-done(((bf16[144,768]{1,0:T(8,128)(2,1)}), bf16[1152,768]{1,0:T(8,128)(2,1)}) %all-gather.11.cloned.1.call-update) | async-done | bytes 1769488 | tf_op jit(solution)/shard_map/all_gather | solution.py:380
  231.9 8.8 %fusion.5 = (bf16[1024,1152]{1,0:T(8,128)(2,1)S(1)}, bf16[1024,1152]{1,0:T(8,128)(2,1)S(1)}, bf16[1024,1152]{1,0:T(8,128)(2,1)}) fusion(f32[1024,2304]{1,0:T(8,128)} %fusion.45, bf16[1152,768]{1,0:T(8,128)(2,1)} %all-gather.11.cloned.1.call-done, bf16[1,1024,768]{2,1,0:T(8,128)(2,1)S(1)} %copy-done.4), kind=kOutput, calls=%fused_computation.12 | convolution fusion | flops 1830813696 | bytes 19857408 | tf_op jit(solution)/shard_map/dot_general | solution.py:351
  240.8 4.4 multiply_reduce_fusion
  245.2 1.3 multiply_add_fusion
  246.5 1.7 copy-done.3
  248.2 2.5 fusion.25
  251.0 4.9 convolution_convert_fusion.2
  256.0 3.1 fusion.34
  259.1 9.2 %convolution_convert_fusion = bf16[768,2304]{1,0:T(8,128)(2,1)} fusion(bf16[1024,1152]{1,0:T(8,128)(2,1)} %copy-done.14, bf16[1024,1152]{1,0:T(8,128)(2,1)} %copy-done.13, f32[1024,768]{1,0:T(8,128)} %copy-done.1, f32[768]{0:T(1024)S(1)} %convert_element_type.152, f32[1024]{0:T(1024)S(1)} %add_rsqrt_fusion.1, f32[1024]{0:T(1024)S(1)} %broadcast_multiply_fusion.5), kind=kOutput, calls=%fused_computation.2 | convolution fusion | flops 3638231040 | bytes 11414528 | tf_op jit(solution)/shard_map/dot_general | solution.py:345
  268.4 1.2 copy-done.10
  269.6 4.5 fusion.29.do_ref
  274.2 98.2 %shard_map.154 = (bf16[1,1024,768]{2,1,0:T(8,128)(2,1)}, bf16[2,1,2048,768]{3,2,1,0:T(8,128)(2,1)}) custom-call(s32[1,4]{1,0:T(1,128)} %get-tuple-element.50.lo_ref, s32[1,4]{1,0:T(1,128)} %get-tuple-element.49.hi_ref, bf16[1,1024,768]{2,1,0:T(8,128)(2,1)} %bitcast.82, bf16[1,2048,1536]{2,1,0:T(8,128)(2,1)} %pad_maximum_fusion.k_ref.v_ref, ...), custom_call_target="tpu_custom_call" | custom-call | flops 32212254720 | bytes 25165824 | tf_op jit(solution)/shard_map/pallas_call | solution.py:272
  372.3 3.8 constant_dynamic-slice_fusion
  376.1 3.8 dynamic-slice_bitcast_fusion.refs_3_
  379.9 2.2 collective-permute-done.1
  382.1 7.1 %shard_map.155 = bf16[1024,2304]{1,0:T(8,128)(2,1)} custom-call(bf16[1024,768]{1,0:T(8,128)(2,1)} %bitcast.75, f32[1024,128]{1,0:T(8,128)} %get-tuple-element.42.cos_ref.refs_1_, f32[1024,128]{1,0:T(8,128)} %get-tuple-element.41.sin_ref.refs_2_, bf16[2,1024,768]{2,1,0:T(8,128)(2,1)} %dynamic-slice_bitcast_fusion.refs_3_, bf16[2,1024,768]{2,1,0:T(8,128)(2,1)} %bitcast.15.refs_4_), custom_call_target="tpu_custom_call" | custom-call | flops 7864320 | bytes 12582912 | tf_op jit(solution)/shard_map/pallas_call | solution.py:330
  389.2 7.7 %convolution_convert_fusion.1 = bf16[768,2304]{1,0:T(8,128)(2,1)} fusion(bf16[1024,768]{1,0:T(8,128)(2,1)S(1)} %copy-done.12, bf16[1024,2304]{1,0:T(8,128)(2,1)} %shard_map.155), kind=kOutput, calls=%fused_computation.3 | convolution fusion | flops 3625648128 | bytes 9830400 | tf_op jit(solution)/shard_map/dot_general | solution.py:345
  398.7 1.5 collective-permute-done.4
  400.1 1.1 add_convert_fusion.4
  401.3 6.9 %fusion.28 = bf16[1,1024,768]{2,1,0:T(8,128)(2,1)} fusion(f32[1024,768]{1,0:T(8,128)} %copy-done.1, bf16[1024,1152]{1,0:T(8,128)(2,1)} %get-tuple-element.36, bf16[1152,768]{1,0:T(8,128)(2,1)} %all-gather.11.cloned.1.call-done), kind=kOutput, calls=%fused_computation.52 | convolution fusion | flops 1813512192 | bytes 8847360 | tf_op jit(solution)/shard_map/dot_general | solution.py:437
  409.0 5.9 %fusion.16 = (f32[768]{0:T(1024)S(1)}, f32[1024]{0:T(1024)S(1)}, f32[1024]{0:T(1024)S(1)}, f32[1024,768]{1,0:T(8,128)}) fusion(f32[1024]{0:T(1024)S(1)} %add_rsqrt_fusion, f32[1024]{0:T(1024)S(1)} %broadcast_multiply_fusion.1, bf16[1,1024,768]{2,1,0:T(8,128)(2,1)S(1)} %copy-done, f32[768]{0:T(1024)S(1)} %convert_element_type.159, ...), kind=kOutput, calls=%fused_computation.29 | convolution fusion | flops 3630953728 | bytes 12998656 | tf_op jit(solution)/shard_map/dot_general | solution.py:351
  415.0 4.7 fusion.15
  419.8 1.7 collective-permute-start.9
  421.4 43.6 %reduce-scatter.9.cloned.1.call-done = bf16[96,2304]{1,0:T(8,128)(2,1)} async-done(((bf16[768,2304]{1,0:T(8,128)(2,1)}), bf16[96,2304]{1,0:T(8,128)(2,1)}) %reduce-scatter.9.cloned.1.call-update) | async-done | bytes 442384 | tf_op jit(solution)/shard_map/reduce_scatter | solution.py:383
  465.0 42.1 %psum.7 = f32[2,768]{1,0:T(2,128)S(1)} all-reduce(f32[2,768]{1,0:T(2,128)S(1)} %pad_maximum_fusion.4), channel_id=1, replica_groups=mesh['fsdp'=8,'rep'=2,'ctx'=2] {'fsdp','rep','ctx'}, use_global_device_ids=true, to_apply=%region_16.17 | all-reduce | flops 1536 | bytes 12288 | tf_op jit(solution)/shard_map/psum | solution.py:477
  508.6 40.2 %reduce-scatter.5.cloned.1.call-done = bf16[96,2304]{1,0:T(8,128)(2,1)} async-done(((bf16[768,2304]{1,0:T(8,128)(2,1)}), bf16[96,2304]{1,0:T(8,128)(2,1)}) %reduce-scatter.5.cloned.1.call-update) | async-done | bytes 442384 | tf_op jit(solution)/shard_map/reduce_scatter | solution.py:383
  548.7 1.1 add_convert_fusion.1
  549.9 1.5 collective-permute-start.7
  551.4 1.1 add_convert_fusion.2
  552.5 0.9 collective-permute-start.3
  553.4 9.6 %collective-permute-done.7 = bf16[96,2304]{1,0:T(8,128)(2,1)S(1)} collective-permute-done((bf16[96,2304]{1,0:T(8,128)(2,1)S(1)}, bf16[96,2304]{1,0:T(8,128)(2,1)S(1)}, u32[]{:S(2)}, u32[]{:S(2)}) %collective-permute-start.7) | collective-permute-done | bytes 442400 | tf_op jit(solution)/shard_map/ppermute | solution.py:375
  563.0 1.0 convert_add_fusion.1
  564.0 8.0 %collective-permute-done.3 = bf16[96,2304]{1,0:T(8,128)(2,1)S(1)} collective-permute-done((bf16[96,2304]{1,0:T(8,128)(2,1)S(1)}, bf16[96,2304]{1,0:T(8,128)(2,1)S(1)}, u32[]{:S(2)}, u32[]{:S(2)}) %collective-permute-start.3) | collective-permute-done | bytes 442400 | tf_op jit(solution)/shard_map/ppermute | solution.py:375
  572.0 1.0 convert_add_fusion.2
  (94 shorter events, 9.2 us)
Async XLA Ops:
  7.2 70.3 %all-gather.5.cloned.1.call-start = ((), (), s32[]{:S(2)}) async-start(), calls=%async_computation.4 | async-start | bytes 3981312 | tf_op jit(solution)/shard_map/all_gather | solution.py:380
  7.9 182.8 %all-gather.7.cloned.1.call-start = ((), (), s32[]{:S(2)}) async-start(), calls=%async_computation.5 | async-start | bytes 1327104 | tf_op jit(solution)/shard_map/all_gather | solution.py:380
  8.6 187.6 %all-gather.9.cloned.1.call-start = ((), (), s32[]{:S(2)}) async-start(), calls=%async_computation.6 | async-start | bytes 3981312 | tf_op jit(solution)/shard_map/all_gather | solution.py:380
  9.4 222.5 %all-gather.11.cloned.1.call-start = ((), (), s32[]{:S(2)}) async-start(), calls=%async_computation.7 | async-start | bytes 1990656 | tf_op jit(solution)/shard_map/all_gather | solution.py:380
  77.5 8.9 %copy-start.7 = (bf16[768]{0:T(1024)(128)(2,1)S(1)}, bf16[768]{0:T(1024)(128)(2,1)}, u32[]{:S(2)}) copy-start(bf16[768]{0:T(1024)(128)(2,1)} %param.15) | copy-start | bytes 4612
  86.4 5.9 %collective-permute-start = (bf16[1,1024,1536]{2,1,0:T(8,128)(2,1)}, bf16[1,1024,1536]{2,1,0:T(8,128)(2,1)S(1)}, u32[]{:S(2)}, u32[]{:S(2)}) collective-permute-start(bf16[1,1024,1536]{2,1,0:T(8,128)(2,1)} %bitcast.74), channel_id=1, source_target_pairs={{0,1},{1,0},{2,3},{3,2},{4,5},{5,4},{6,7},{7,6},{8,9},{9,8},{10,11... | collective-permute-start | bytes 9437192 | tf_op jit(solution)/shard_map/ppermute | solution.py:419
  86.4 312.1 %reduce-scatter.7.cloned.1.call-start = ((), (), s32[]{:S(2)}) async-start(), calls=%async_computation.9 | async-start | bytes 1327104 | tf_op jit(solution)/shard_map/reduce_scatter | solution.py:383
  97.6 93.1 %copy-start = (bf16[1,1024,768]{2,1,0:T(8,128)(2,1)S(1)}, bf16[1,1024,768]{2,1,0:T(8,128)(2,1)}, u32[]{:S(2)}) copy-start(bf16[1,1024,768]{2,1,0:T(8,128)(2,1)} %param.9) | copy-start | bytes 4718596
  194.0 1.7 copy-start.1
  196.2 35.7 %copy-start.4 = (bf16[1,1024,768]{2,1,0:T(8,128)(2,1)S(1)}, bf16[1,1024,768]{2,1,0:T(8,128)(2,1)}, u32[]{:S(2)}) copy-start(bf16[1,1024,768]{2,1,0:T(8,128)(2,1)} %param.10) | copy-start | bytes 4718596
  231.9 8.8 %copy-start.2 = (f32[1024,768]{1,0:T(8,128)S(1)}, f32[1024,768]{1,0:T(8,128)}, u32[]{:S(2)}) copy-start(f32[1024,768]{1,0:T(8,128)} %copy-done.1) | copy-start | bytes 9437188
  231.9 8.8 %copy-start.9 = (bf16[768,2304]{1,0:T(8,128)(2,1)S(1)}, bf16[768,2304]{1,0:T(8,128)(2,1)}, u32[]{:S(2)}) copy-start(bf16[768,2304]{1,0:T(8,128)(2,1)} %all-gather.9.cloned.1.call-done) | copy-start | bytes 10616836
  240.7 4.4 copy-start.13
  240.7 4.4 copy-start.14
  245.2 3.0 copy-start.11
  246.5 1.7 copy-start.3
  250.7 164.1 %reduce-scatter.11.cloned.1.call-start = ((), (), s32[]{:S(2)}) async-start(), calls=%async_computation.11 | async-start | bytes 1990656 | tf_op jit(solution)/shard_map/reduce_scatter | solution.py:383
  256.0 209.0 %reduce-scatter.9.cloned.1.call-start = ((), (), s32[]{:S(2)}) async-start(), calls=%async_computation.10 | async-start | bytes 3981312 | tf_op jit(solution)/shard_map/reduce_scatter | solution.py:383
  268.4 1.3 copy-start.10
  268.4 280.3 %reduce-scatter.5.cloned.1.call-start = ((), (), s32[]{:S(2)}) async-start(), calls=%async_computation.8 | async-start | bytes 3981312 | tf_op jit(solution)/shard_map/reduce_scatter | solution.py:383
  376.1 6.0 %collective-permute-start.1 = (bf16[2,1,1024,768]{3,2,0,1:T(8,128)(2,1)}, bf16[2,1,1024,768]{3,2,0,1:T(8,128)(2,1)}, u32[]{:S(2)}, u32[]{:S(2)}) collective-permute-start(bf16[2,1,1024,768]{3,2,0,1:T(8,128)(2,1)} %constant_dynamic-slice_fusion), channel_id=1, source_target_pairs={{0,1},{1,0},{2,3},{3,2},{4,5},{5,4},{6,7},{7,6},{8,9},{9,8},{10,11... | collective-permute-start | bytes 9437192 | tf_op jit(solution)/shard_map/ppermute | solution.py:464
  382.1 7.1 %copy-start.12 = (bf16[1024,768]{1,0:T(8,128)(2,1)S(1)}, bf16[1024,768]{1,0:T(8,128)(2,1)}, u32[]{:S(2)}) copy-start(bf16[1024,768]{1,0:T(8,128)(2,1)} %get-tuple-element.21) | copy-start | bytes 4718596
  396.9 0.7 copy-start.6
  398.5 1.6 collective-permute-start.4
  400.1 8.8 %slice-start = ((s8[4718592]{0:T(1024)(128)(4,1)}), s8[4194304]{0:T(1024)(128)(4,1)S(1)}, s32[]{:S(2)}) async-start(s8[4718592]{0:T(1024)(128)(4,1)} %bitcast.72), calls=%async_computation.12 | async-start | bytes 8388608
  401.2 7.7 %slice-start.1 = ((s8[4718592]{0:T(1024)(128)(4,1)}), s8[524288]{0:T(1024)(128)(4,1)S(1)}, s32[]{:S(2)}) async-start(s8[4718592]{0:T(1024)(128)(4,1)} %bitcast.72), calls=%async_computation.13 | async-start | bytes 1048576
  401.2 7.7 %copy-start.8 = (bf16[768,2304]{1,0:T(8,128)(2,1)S(1)}, bf16[768,2304]{1,0:T(8,128)(2,1)}, u32[]{:S(2)}) copy-start(bf16[768,2304]{1,0:T(8,128)(2,1)} %all-gather.5.cloned.1.call-done.w_ref) | copy-start | bytes 10616836
  401.3 7.0 %collective-permute-start.5 = (bf16[96,768]{1,0:T(8,128)(2,1)S(1)}, bf16[96,768]{1,0:T(8,128)(2,1)S(1)}, u32[]{:S(2)}, u32[]{:S(2)}) collective-permute-start(bf16[96,768]{1,0:T(8,128)(2,1)S(1)} %add_convert_fusion.4), channel_id=1, source_target_pairs={{0,2},{2,0},{1,3},{3,1},{4,6},{6,4},{5,7},{7,5},{8,10},{10,8},{9,1... | collective-permute-start | bytes 442376 | tf_op jit(solution)/shard_map/ppermute | solution.py:375
  414.9 4.8 collective-permute-start.8
  415.0 4.7 copy-start.5
  419.8 88.0 %collective-permute-start.9 = (bf16[144,768]{1,0:T(8,128)(2,1)S(1)}, bf16[144,768]{1,0:T(8,128)(2,1)S(1)}, u32[]{:S(2)}, u32[]{:S(2)}) collective-permute-start(bf16[144,768]{1,0:T(8,128)(2,1)S(1)} %add_convert_fusion.3), channel_id=1, source_target_pairs={{0,2},{2,0},{1,3},{3,1},{4,6},{6,4},{5,7},{7,5},{8,10},{10,8},{9,1... | collective-permute-start | bytes 663560 | tf_op jit(solution)/shard_map/ppermute | solution.py:375
  465.0 83.8 %collective-permute-start.6 = (bf16[96,2304]{1,0:T(8,128)(2,1)}, bf16[96,2304]{1,0:T(8,128)(2,1)S(1)}, u32[]{:S(2)}, u32[]{:S(2)}) collective-permute-start(bf16[96,2304]{1,0:T(8,128)(2,1)} %reduce-scatter.9.cloned.1.call-done), channel_id=1, source_target_pairs={{0,1},{1,0},{2,3},{3,2},{4,5},{5,4},{6,7},{7,6},{8,9},{9,8},{10,11... | collective-permute-start | bytes 1327112 | tf_op jit(solution)/shard_map/ppermute | solution.py:375
  548.7 2.7 collective-permute-start.2
  549.9 13.1 %collective-permute-start.7 = (bf16[96,2304]{1,0:T(8,128)(2,1)S(1)}, bf16[96,2304]{1,0:T(8,128)(2,1)S(1)}, u32[]{:S(2)}, u32[]{:S(2)}) collective-permute-start(bf16[96,2304]{1,0:T(8,128)(2,1)S(1)} %add_convert_fusion.1), channel_id=1, source_target_pairs={{0,2},{2,0},{1,3},{3,1},{4,6},{6,4},{5,7},{7,5},{8,10},{10,8},{9,1... | collective-permute-start | bytes 1327112 | tf_op jit(solution)/shard_map/ppermute | solution.py:375
  552.5 19.5 %collective-permute-start.3 = (bf16[96,2304]{1,0:T(8,128)(2,1)S(1)}, bf16[96,2304]{1,0:T(8,128)(2,1)S(1)}, u32[]{:S(2)}, u32[]{:S(2)}) collective-permute-start(bf16[96,2304]{1,0:T(8,128)(2,1)S(1)} %add_convert_fusion.2), channel_id=1, source_target_pairs={{0,2},{2,0},{1,3},{3,1},{4,6},{6,4},{5,7},{7,5},{8,10},{10,8},{9,1... | collective-permute-start | bytes 1327112 | tf_op jit(solution)/shard_map/ppermute | solution.py:375
Sparse Core Ops, SparseCore 0:
  10.2 67.3 all-gather.4
  79.7 40.1 all-gather.6
  122.1 63.0 all-gather.8
  187.2 44.6 all-gather.10
  250.9 63.2 reduce-scatter.6
  317.4 65.6 reduce-scatter.10
  386.8 78.1 reduce-scatter.8
  468.6 80.0 reduce-scatter.4
